TPU v7x, 256 devices: a whole 4x4x8 slice. The times are simulated.
256 devices in a mesh: table: 16 (over x, y), dp: 8 (over z), col: 2 (over core).
Axes of the slice: x: 4, y: 4, z: 8, core: 2. Of those that a mesh axis runs over, the one named last changes fastest.
Arguments:
- table_weights: float32 [32768, 512], P('table', 'col'), may hold values from -6 to 6
- moment_first: float32 [32768, 512], P('table', 'col'), may hold values from -3 to 3
- moment_second: float32 [32768], P('table'), may hold values from 0.1 to 2
- hot_slices: int32 [16, 2], replicated, may hold values from 0 to 31, as said below
- upstream_grad: bfloat16 [131072, 512], P(('table', 'dp'), 'col'), may hold values from -20 to 20
- dedup_map: int32 [131072, 32], P(('table', 'dp')), may hold values from 0 to 4095, as said below
- unique_rows: int32 [128, 16, 256], P(('table', 'dp')), may hold values from 0 to 32767, as said below
- row_counts: int32 [128, 16], P(('table', 'dp')), may hold values from 192 to 256, as said below
Outputs:
- new_weights: float32 [32768, 512], P('table', 'col')
- new_first: float32 [32768, 512], P('table', 'col')
- new_second: float32 [32768], P('table')
Inputs may be any that keep to these rules, and one draw needn't show every extreme that they name: `hot_slices`: each row holds 2 different slice numbers below 32. `unique_rows`: for source device s and owner t, the first row_counts[s, t] entries are different rows r with physical(r) on table index t; the remaining entries are not used. `row_counts`: in every draw some owner receives 256 used slots from every source device. `dedup_map`: an entry in a row of source device s is a used slot t * 256 + k with k < row_counts[s, t].
All inputs are finite; a program needn't handle non-finite values.
Results may differ from a plain program's by a relative error of at most 0.0003.
Values sent between devices are 32-bit elements; how exact they have to be, the bound alone decides.
No kernel may reach another device: no remote copies, remote signals or barrier semaphores. Data moves between devices by JAX's collectives and lax.ppermute only.
A program may use at most 64 MiB of HBM per device.

v0:
```python
import jax
import jax.numpy as jnp
from jax import lax
from jax.sharding import PartitionSpec as P

SLICE = 64
beta_one = 0.9
beta_two = 0.99
learn_rate = 0.1
eps_value = 1e-08


def partner_2(block, axis, distance):
    count = lax.axis_size(axis)
    route = []
    for low in range(count):
        high = low | 1 << distance
        if high != low and high < count:
            route += [(low, high), (high, low)]
    return lax.ppermute(block, axis, route)


def local_targets(logical_rows, hot_slices, rows_dev):
    n_table = hot_slices.shape[0]
    row_owner = logical_rows // rows_dev
    local_row = logical_rows % rows_dev
    row_piece = local_row // SLICE
    row_offset = local_row % SLICE
    matches = hot_slices[row_owner] == row_piece[..., None]
    partner = (row_owner + n_table // 2) % n_table
    partner_piece = jnp.sum(jnp.where(matches, hot_slices[partner], 0), axis=-1)
    return jnp.where(jnp.any(matches, axis=-1), partner_piece * SLICE + row_offset, local_row)


def adam_rows(weights, first, second, gradient, squares, full_width):
    new_second = beta_two * second + (1.0 - beta_two) * (squares / full_width)
    new_first = beta_one * first + (1.0 - beta_one) * gradient
    scaled = jnp.sqrt(new_second / (1.0 - beta_two**8)) + eps_value
    new_weights = weights - learn_rate * (new_first / (1.0 - beta_one**8)) / scaled[:, None]
    return (new_weights, new_first, new_second)


def on_device(
    table_weights,
    moment_first,
    moment_second,
    hot_slices,
    upstream_grad,
    dedup_map,
    unique_rows,
    row_counts,
):
    n_table = lax.axis_size("table")
    position = lax.axis_index("table")
    rows_dev, col_width = table_weights.shape
    own_hot = hot_slices[position]
    n_hots = own_hot.shape[0]
    starts = [own_hot[k] * SLICE for k in range(n_hots)]
    out_weights = jnp.stack(
        [lax.dynamic_slice_in_dim(table_weights, starts[k], SLICE, 0) for k in range(n_hots)]
    )
    out_first = jnp.stack(
        [lax.dynamic_slice_in_dim(moment_first, starts[k], SLICE, 0) for k in range(n_hots)]
    )
    out_second = jnp.stack(
        [lax.dynamic_slice_in_dim(moment_second, starts[k], SLICE, 0) for k in range(n_hots)]
    )
    swap_bit = n_table.bit_length() - 2
    incoming = partner_2((out_weights, out_first, out_second), "table", swap_bit)
    placed_weights = table_weights
    placed_first = moment_first
    placed_second = moment_second
    for k in range(n_hots):
        placed_weights = lax.dynamic_update_slice_in_dim(
            placed_weights, incoming[0][k], starts[k], 0
        )
        placed_first = lax.dynamic_update_slice_in_dim(placed_first, incoming[1][k], starts[k], 0)
        placed_second = lax.dynamic_update_slice_in_dim(placed_second, incoming[2][k], starts[k], 0)
    slot_cap = unique_rows.shape[2]
    valid = jnp.arange(slot_cap)[None, :] < row_counts[0][:, None]
    targets = jnp.where(valid, local_targets(unique_rows[0], hot_slices, rows_dev), rows_dev)
    slot_iota = jnp.arange(slot_cap)

    def owner_block(carry, owner):
        wanted = slot_iota + owner * slot_cap
        tally = jnp.sum(
            (dedup_map[None, :, :] == wanted[:, None, None]).astype(jnp.float32), axis=2
        )
        block = jnp.dot(
            tally.astype(jnp.bfloat16), upstream_grad, preferred_element_type=jnp.float32
        )
        return (carry, block)

    _, slot_grad = lax.scan(owner_block, 0, jnp.arange(n_table))
    got_grad, got_target = (
        lax.all_to_all(slot_grad, "table", split_axis=0, concat_axis=0, tiled=True),
        lax.all_to_all(targets, "table", split_axis=0, concat_axis=0, tiled=True),
    )
    row_iota = jnp.arange(rows_dev)

    def add_source(total, inputs):
        grad_block, target_block = inputs
        select = (row_iota[:, None] == target_block[None, :]).astype(jnp.float32)
        return (
            total
            + jnp.dot(
                select,
                grad_block,
                precision=lax.Precision.HIGHEST,
                preferred_element_type=jnp.float32,
            ),
            None,
        )

    dense, _ = lax.scan(
        add_source, jnp.zeros((rows_dev, col_width), jnp.float32), (got_grad, got_target)
    )
    full_width = col_width * lax.axis_size("col")
    gradient = lax.psum(dense, "dp")
    squares = lax.psum(jnp.sum(gradient * gradient, axis=1), "col")
    new_weights, new_first, new_second = adam_rows(
        placed_weights, placed_first, placed_second, gradient, squares, full_width
    )
    return (new_weights, new_first, new_second)


def solution(mesh):
    placed = (
        P("table", "col"),
        P("table", "col"),
        P("table"),
        P(),
        P(("table", "dp"), "col"),
        P(("table", "dp"), None),
        P(("table", "dp"), None, None),
        P(("table", "dp"), None),
    )
    return jax.shard_map(
        on_device,
        mesh=mesh,
        in_specs=placed,
        out_specs=(P("table", "col"), P("table", "col"), P("table")),
        check_vma=False,
    )
```

profile of v0, /device:TPU:1, one launch (start us, length us, event | category | flops | bytes accessed | tf_op | source)
XLA Modules:
  0.0 479.1 jit_solution(15004162492710192044)
XLA Ops:
  7.2 3.2 copy.52
  11.9 10.8 %gather_fusion = s32[4096,2]{1,0:T(8,128)S(1)} fusion(s32[16,2]{1,0:T(8,128)S(1)} %copy.21, s32[4096]{0:T(1024)S(1)} %broadcast_clamp_fusion.1), kind=kCustom, calls=%fused_computation | custom fusion | bytes 81920 | tf_op jit(solution)/shard_map/gather | solution.py:29
  22.7 14.1 %gather_fusion.1 = s32[4096,2]{1,0:T(8,128)} fusion(s32[16,2]{1,0:T(8,128)S(1)} %copy.21, s32[4096]{0:T(1024)S(1)} %broadcast_clamp_fusion), kind=kCustom, calls=%fused_computation.1 | custom fusion | bytes 81920 | tf_op jit(solution)/shard_map/gather | solution.py:31
  39.8 7.6 %all-to-all-start = ((s32[16,1,256]{2,1,0:T(1,128)}), s32[16,1,256]{2,1,0:T(1,128)S(1)}, u32[]{:S(2)}, u32[]{:S(2)}) async-start(s32[16,1,256]{2,1,0:T(1,128)} %copy.23), calls=%async_computation | async-start | bytes 32768 | tf_op jit(solution)/shard_map/all_to_all | solution.py:97
  47.4 217.9 %while.22 = (s32[]{:T(128)}, f32[16,256,256]{2,1,0:T(8,128)}, s32[1024,32]{0,1:T(8,128)S(1)}, s32[16]{0:T(128)S(1)}, bf16[1024,256]{1,0:T(8,128)(2,1)S(1)}, /*index=5*/s32[]{:T(128)}, s32[1]{0:T(128)}) while((s32[]{:T(128)}, f32[16,256,256]{2,1,0:T(8,128)}, s32[1024,32]{0,1:T(8,128)S(1)}, s32[16]{0:T(128)S(1)}, ...), condition=%wide.region_2.3_spmd.clone, body=%wide.region_0.2_spmd.clone.sunk | while | flops 159121664 | bytes 1968745 | solution.py:94
  48.9 11.3 %convert_reduce_fusion.2 = bf16[256,1024]{1,0:T(8,128)(2,1)S(1)} fusion(s32[1024,32]{0,1:T(8,128)S(1)} %get-tuple-element.201, s32[256]{0:T(256)S(1)} %iota_add_fusion.2), kind=kLoop, calls=%fused_computation.4.clone.1 | loop fusion | flops 24903680 | bytes 656384 | tf_op jit(solution)/shard_map/while/body/eval_jaxpr/reduce_sum | solution.py:86
  62.5 11.3 %convert_reduce_fusion.2 = bf16[256,1024]{1,0:T(8,128)(2,1)S(1)} fusion(s32[1024,32]{0,1:T(8,128)S(1)} %get-tuple-element.201, s32[256]{0:T(256)S(1)} %iota_add_fusion.2), kind=kLoop, calls=%fused_computation.4.clone.1 | loop fusion | flops 24903680 | bytes 656384 | tf_op jit(solution)/shard_map/while/body/eval_jaxpr/reduce_sum | solution.py:86
  76.1 11.3 %convert_reduce_fusion.2 = bf16[256,1024]{1,0:T(8,128)(2,1)S(1)} fusion(s32[1024,32]{0,1:T(8,128)S(1)} %get-tuple-element.201, s32[256]{0:T(256)S(1)} %iota_add_fusion.2), kind=kLoop, calls=%fused_computation.4.clone.1 | loop fusion | flops 24903680 | bytes 656384 | tf_op jit(solution)/shard_map/while/body/eval_jaxpr/reduce_sum | solution.py:86
  89.7 11.3 %convert_reduce_fusion.2 = bf16[256,1024]{1,0:T(8,128)(2,1)S(1)} fusion(s32[1024,32]{0,1:T(8,128)S(1)} %get-tuple-element.201, s32[256]{0:T(256)S(1)} %iota_add_fusion.2), kind=kLoop, calls=%fused_computation.4.clone.1 | loop fusion | flops 24903680 | bytes 656384 | tf_op jit(solution)/shard_map/while/body/eval_jaxpr/reduce_sum | solution.py:86
  103.3 11.3 %convert_reduce_fusion.2 = bf16[256,1024]{1,0:T(8,128)(2,1)S(1)} fusion(s32[1024,32]{0,1:T(8,128)S(1)} %get-tuple-element.201, s32[256]{0:T(256)S(1)} %iota_add_fusion.2), kind=kLoop, calls=%fused_computation.4.clone.1 | loop fusion | flops 24903680 | bytes 656384 | tf_op jit(solution)/shard_map/while/body/eval_jaxpr/reduce_sum | solution.py:86
  116.9 11.3 %convert_reduce_fusion.2 = bf16[256,1024]{1,0:T(8,128)(2,1)S(1)} fusion(s32[1024,32]{0,1:T(8,128)S(1)} %get-tuple-element.201, s32[256]{0:T(256)S(1)} %iota_add_fusion.2), kind=kLoop, calls=%fused_computation.4.clone.1 | loop fusion | flops 24903680 | bytes 656384 | tf_op jit(solution)/shard_map/while/body/eval_jaxpr/reduce_sum | solution.py:86
  130.5 11.3 %convert_reduce_fusion.2 = bf16[256,1024]{1,0:T(8,128)(2,1)S(1)} fusion(s32[1024,32]{0,1:T(8,128)S(1)} %get-tuple-element.201, s32[256]{0:T(256)S(1)} %iota_add_fusion.2), kind=kLoop, calls=%fused_computation.4.clone.1 | loop fusion | flops 24903680 | bytes 656384 | tf_op jit(solution)/shard_map/while/body/eval_jaxpr/reduce_sum | solution.py:86
  144.1 11.3 %convert_reduce_fusion.2 = bf16[256,1024]{1,0:T(8,128)(2,1)S(1)} fusion(s32[1024,32]{0,1:T(8,128)S(1)} %get-tuple-element.201, s32[256]{0:T(256)S(1)} %iota_add_fusion.2), kind=kLoop, calls=%fused_computation.4.clone.1 | loop fusion | flops 24903680 | bytes 656384 | tf_op jit(solution)/shard_map/while/body/eval_jaxpr/reduce_sum | solution.py:86
  157.7 11.3 %convert_reduce_fusion.2 = bf16[256,1024]{1,0:T(8,128)(2,1)S(1)} fusion(s32[1024,32]{0,1:T(8,128)S(1)} %get-tuple-element.201, s32[256]{0:T(256)S(1)} %iota_add_fusion.2), kind=kLoop, calls=%fused_computation.4.clone.1 | loop fusion | flops 24903680 | bytes 656384 | tf_op jit(solution)/shard_map/while/body/eval_jaxpr/reduce_sum | solution.py:86
  171.3 11.3 %convert_reduce_fusion.2 = bf16[256,1024]{1,0:T(8,128)(2,1)S(1)} fusion(s32[1024,32]{0,1:T(8,128)S(1)} %get-tuple-element.201, s32[256]{0:T(256)S(1)} %iota_add_fusion.2), kind=kLoop, calls=%fused_computation.4.clone.1 | loop fusion | flops 24903680 | bytes 656384 | tf_op jit(solution)/shard_map/while/body/eval_jaxpr/reduce_sum | solution.py:86
  184.9 11.3 %convert_reduce_fusion.2 = bf16[256,1024]{1,0:T(8,128)(2,1)S(1)} fusion(s32[1024,32]{0,1:T(8,128)S(1)} %get-tuple-element.201, s32[256]{0:T(256)S(1)} %iota_add_fusion.2), kind=kLoop, calls=%fused_computation.4.clone.1 | loop fusion | flops 24903680 | bytes 656384 | tf_op jit(solution)/shard_map/while/body/eval_jaxpr/reduce_sum | solution.py:86
  198.5 11.3 %convert_reduce_fusion.2 = bf16[256,1024]{1,0:T(8,128)(2,1)S(1)} fusion(s32[1024,32]{0,1:T(8,128)S(1)} %get-tuple-element.201, s32[256]{0:T(256)S(1)} %iota_add_fusion.2), kind=kLoop, calls=%fused_computation.4.clone.1 | loop fusion | flops 24903680 | bytes 656384 | tf_op jit(solution)/shard_map/while/body/eval_jaxpr/reduce_sum | solution.py:86
  212.1 11.3 %convert_reduce_fusion.2 = bf16[256,1024]{1,0:T(8,128)(2,1)S(1)} fusion(s32[1024,32]{0,1:T(8,128)S(1)} %get-tuple-element.201, s32[256]{0:T(256)S(1)} %iota_add_fusion.2), kind=kLoop, calls=%fused_computation.4.clone.1 | loop fusion | flops 24903680 | bytes 656384 | tf_op jit(solution)/shard_map/while/body/eval_jaxpr/reduce_sum | solution.py:86
  225.7 11.3 %convert_reduce_fusion.2 = bf16[256,1024]{1,0:T(8,128)(2,1)S(1)} fusion(s32[1024,32]{0,1:T(8,128)S(1)} %get-tuple-element.201, s32[256]{0:T(256)S(1)} %iota_add_fusion.2), kind=kLoop, calls=%fused_computation.4.clone.1 | loop fusion | flops 24903680 | bytes 656384 | tf_op jit(solution)/shard_map/while/body/eval_jaxpr/reduce_sum | solution.py:86
  239.3 11.3 %convert_reduce_fusion.2 = bf16[256,1024]{1,0:T(8,128)(2,1)S(1)} fusion(s32[1024,32]{0,1:T(8,128)S(1)} %get-tuple-element.201, s32[256]{0:T(256)S(1)} %iota_add_fusion.2), kind=kLoop, calls=%fused_computation.4.clone.1 | loop fusion | flops 24903680 | bytes 656384 | tf_op jit(solution)/shard_map/while/body/eval_jaxpr/reduce_sum | solution.py:86
  252.9 11.3 %convert_reduce_fusion.2 = bf16[256,1024]{1,0:T(8,128)(2,1)S(1)} fusion(s32[1024,32]{0,1:T(8,128)S(1)} %get-tuple-element.201, s32[256]{0:T(256)S(1)} %iota_add_fusion.2), kind=kLoop, calls=%fused_computation.4.clone.1 | loop fusion | flops 24903680 | bytes 656384 | tf_op jit(solution)/shard_map/while/body/eval_jaxpr/reduce_sum | solution.py:86
  265.3 6.7 %all-to-all-start.1 = ((f32[16,256,256]{2,1,0:T(8,128)}), f32[16,256,256]{2,1,0:T(8,128)}, u32[]{:S(2)}, u32[]{:S(2)}) async-start(f32[16,256,256]{2,1,0:T(8,128)} %get-tuple-element.62), calls=%async_computation.1 | async-start | bytes 8388608 | tf_op jit(solution)/shard_map/all_to_all | solution.py:96
  272.1 51.8 %all-to-all-done.1 = f32[16,256,256]{2,1,0:T(8,128)} async-done(((f32[16,256,256]{2,1,0:T(8,128)}), f32[16,256,256]{2,1,0:T(8,128)}, u32[]{:S(2)}, u32[]{:S(2)}) %all-to-all-start.1) | async-done | bytes 4194336 | tf_op jit(solution)/shard_map/all_to_all | solution.py:96
  323.9 45.4 %while.23 = (s32[]{:T(128)}, f32[2048,256]{1,0:T(8,128)S(1)}, s32[16,256]{1,0:T(8,128)S(1)}, f32[16,256,256]{2,1,0:T(8,128)}, s32[]{:T(128)}, /*index=5*/s32[]{:T(128)}) while((s32[]{:T(128)}, f32[2048,256]{1,0:T(8,128)S(1)}, s32[16,256]{1,0:T(8,128)S(1)}, f32[16,256,256]{2,1,0:T(8,128)}, s32[]{:T(128)}, /*index=5*/s32[]{:T(128)}) %tuple.62), condition=%wide.region_6.7_spmd.clone, body=%wide.region_5.6_spmd.clone.sunk | while | flops 1612185600 | bytes 4460115 | solution.py:115
  326.7 2.8 convolution_add_fusion.2
  329.6 2.8 convolution_add_fusion.2
  340.9 2.8 convolution_add_fusion.2
  373.5 4.6 collective-permute-start.1
  378.2 3.0 collective-permute-start
  386.2 73.0 %all-reduce.2.cloned.1.call-done = f32[2048,256]{1,0:T(8,128)} async-done(((f32[2048,256]{1,0:T(8,128)}), f32[2048,256]{1,0:T(8,128)}) %all-reduce.2.cloned.1.call-update) | async-done | bytes 2097168 | tf_op jit(solution)/shard_map/psum | solution.py:119
  461.1 5.8 %psum.15 = f32[2048]{0:T(1024)S(1)} all-reduce(f32[2048]{0:T(1024)S(1)} %multiply_reduce_fusion), channel_id=1, replica_groups=mesh['table'=16,'dp'=8,'col'=2] {'col'}, use_global_device_ids=true, to_apply=%region_9.10 | all-reduce | flops 2048 | bytes 16384 | tf_op jit(solution)/shard_map/psum | solution.py:120
  467.5 4.8 divide_subtract_fusion
  (136 shorter events, 77.5 us)
Async XLA Ops:
  7.2 3.2 copy-start.5
  10.4 1.3 copy-start.7
  10.4 1.3 copy-start.6
  10.4 1.4 copy-start.8
  36.8 1.6 copy-start.3
  36.8 2.3 copy-start.9
  36.8 10.6 %copy-start.1 = (bf16[1024,256]{1,0:T(8,128)(2,1)S(1)}, bf16[1024,256]{1,0:T(8,128)(2,1)}, u32[]{:S(2)}) copy-start(bf16[1024,256]{1,0:T(8,128)(2,1)} %param.16) | copy-start | bytes 1572868
  36.8 10.6 %copy-start.4 = (s32[1024,32]{0,1:T(8,128)S(1)}, s32[1024,32]{0,1:T(8,128)}, u32[]{:S(2)}) copy-start(s32[1024,32]{0,1:T(8,128)} %param.17) | copy-start | bytes 393220
  39.8 225.5 %all-to-all-start = ((s32[16,1,256]{2,1,0:T(1,128)}), s32[16,1,256]{2,1,0:T(1,128)S(1)}, u32[]{:S(2)}, u32[]{:S(2)}) async-start(s32[16,1,256]{2,1,0:T(1,128)} %copy.23), calls=%async_computation | async-start | bytes 32768 | tf_op jit(solution)/shard_map/all_to_all | solution.py:97
  265.3 58.6 %all-to-all-start.1 = ((f32[16,256,256]{2,1,0:T(8,128)}), f32[16,256,256]{2,1,0:T(8,128)}, u32[]{:S(2)}, u32[]{:S(2)}) async-start(f32[16,256,256]{2,1,0:T(8,128)} %get-tuple-element.62), calls=%async_computation.1 | async-start | bytes 8388608 | tf_op jit(solution)/shard_map/all_to_all | solution.py:96
  272.0 187.1 %all-reduce.2.cloned.1.call-start = ((), (), s32[]{:S(2)}) async-start(), calls=%async_computation.2 | async-start | bytes 4194304 | tf_op jit(solution)/shard_map/psum | solution.py:119
  369.3 1.3 copy-start
  373.5 9.1 %collective-permute-start.1 = (f32[2,64,256]{2,1,0:T(8,128)S(1)}, f32[2,64,256]{2,1,0:T(8,128)S(1)}, u32[]{:S(2)}, u32[]{:S(2)}) collective-permute-start(f32[2,64,256]{2,1,0:T(8,128)S(1)} %pad_maximum_fusion.1), channel_id=1, source_target_pairs={{0,128},{128,0},{16,144},{144,16},{32,160},{160,32},{48,176},{176,... | collective-permute-start | bytes 393224 | tf_op jit(solution)/shard_map/ppermute | solution.py:20
  378.1 4.3 collective-permute-start.2
  378.2 6.7 %collective-permute-start = (f32[2,64,256]{2,1,0:T(8,128)S(1)}, f32[2,64,256]{2,1,0:T(8,128)S(1)}, u32[]{:S(2)}, u32[]{:S(2)}) collective-permute-start(f32[2,64,256]{2,1,0:T(8,128)S(1)} %pad_maximum_fusion), channel_id=1, source_target_pairs={{0,128},{128,0},{16,144},{144,16},{32,160},{160,32},{48,176},{176,... | collective-permute-start | bytes 393224 | tf_op jit(solution)/shard_map/ppermute | solution.py:20
  386.2 81.4 %copy-start.2 = (f32[2048,256]{1,0:T(8,128)S(1)}, f32[2048,256]{1,0:T(8,128)}, u32[]{:S(2)}) copy-start(f32[2048,256]{1,0:T(8,128)} %fusion.12) | copy-start | bytes 6291460
Sparse Core Ops, SparseCore 0:
  370.8 88.3 all-reduce.1
where the time goes:
time: 480 us; the launch traced here: 479 us
  other arithmetic  191 us (40%)
  waiting for transfers between devices  127 us (26%)
  matrix products  60.9 us (13%)
  local copies, waits for them, and re-layouts  45.9 us (10%)
  starting transfers between devices  22 us (5%)
  between operations  15.5 us (3%)
  loops' own time  11.2 us (2%)
  blocking collectives  5.83 us (1%)
    reduce_sum x16, other arithmetic, owner_block(): jnp.sum((dedup_map[None, :, :] == wanted[:, None, None]).astype(jnp.float...  181 us
    psum x1, waiting for transfers between devices, on_device(): gradient = lax.psum(dense, 'dp')  73 us
    all_to_all x1, waiting for transfers between devices, on_device(): lax.all_to_all(slot_grad, 'table', split_axis=0, concat_axis=0, tiled=True)  51.8 us
    dot_general x16, matrix products, add_source(): jnp.dot(select, grad_block, precision=lax.Precision.HIGHEST, preferred_el...  44.7 us
    dot_general x16, matrix products, owner_block(): jnp.dot(tally.astype(jnp.bfloat16), upstream_grad, preferred_element_type...  16.2 us
    gather x1, local copies, waits for them, and re-layouts, local_targets(): partner_piece = jnp.sum(jnp.where(matches, hot_slices[partner], 0), axis=-1)  14.1 us
    gather x1, local copies, waits for them, and re-layouts, local_targets(): matches = hot_slices[row_owner] == row_piece[..., None]  10.8 us
    another operation x1, loops' own time, on_device(): _, slot_grad = lax.scan(owner_block, 0, jnp.arange(n_table))  10.7 us
  transfers between devices with their start and end apart: 6, of which 4 were waited for; matrix products, arithmetic and copies ran while one was open for 44% of the time, Pallas kernels for 0%

commit v1 on v0

--- a/solution.py
+++ b/solution.py
@@ -116,7 +116,8 @@
         add_source, jnp.zeros((rows_dev, col_width), jnp.float32), (got_grad, got_target)
     )
     full_width = col_width * lax.axis_size("col")
-    gradient = lax.psum(dense, "dp")
+    blocks = lax.all_gather(dense, "dp", axis=0, tiled=False)
+    gradient = blocks.sum(axis=0)
     squares = lax.psum(jnp.sum(gradient * gradient, axis=1), "col")
     new_weights, new_first, new_second = adam_rows(
         placed_weights, placed_first, placed_second, gradient, squares, full_width

time: 480 us -> 577 us (1.20)
  waiting for transfers between devices: 127 us -> 221 us
    all_gather x0 -> x1, waiting for transfers between devices: none -> 166 us  [on_device(): blocks = lax.all_gather(dense, 'dp', axis=0, tiled=False)]
    psum x1 -> x0, waiting for transfers between devices: 73 us -> none  [on_device(): gradient = lax.psum(dense, 'dp')]
    reduce_sum x0 -> x1, other arithmetic: none -> 7.14 us  [on_device(): gradient = blocks.sum(axis=0)]
  transfers between devices with their start and end apart: 6 -> 6, of which waited for: 4 -> 4; matrix products, arithmetic and copies ran while one was open for 44% -> 37% of each run, Pallas kernels for 0% -> 0%
where the time goes in v1:
time: 577 us; the launch traced here: 576 us
  waiting for transfers between devices  221 us (38%)
  other arithmetic  196 us (34%)
  matrix products  61 us (11%)
  local copies, waits for them, and re-layouts  46.7 us (8%)
  starting transfers between devices  22.1 us (4%)
  between operations  15.6 us (3%)
  loops' own time  11.2 us (2%)
    reduce_sum x16, other arithmetic, owner_block(): jnp.sum((dedup_map[None, :, :] == wanted[:, None, None]).astype(jnp.float...  181 us
    all_gather x1, waiting for transfers between devices, on_device(): blocks = lax.all_gather(dense, 'dp', axis=0, tiled=False)  166 us
    all_to_all x1, waiting for transfers between devices, on_device(): lax.all_to_all(slot_grad, 'table', split_axis=0, concat_axis=0, tiled=True)  51.8 us
    dot_general x16, matrix products, add_source(): jnp.dot(select, grad_block, precision=lax.Precision.HIGHEST, preferred_el...  44.7 us
    dot_general x16, matrix products, owner_block(): jnp.dot(tally.astype(jnp.bfloat16), upstream_grad, preferred_element_type...  16.2 us
    gather x1, local copies, waits for them, and re-layouts, local_targets(): partner_piece = jnp.sum(jnp.where(matches, hot_slices[partner], 0), axis=-1)  14.1 us
  transfers between devices with their start and end apart: 6, of which 4 were waited for; matrix products, arithmetic and copies ran while one was open for 37% of the time, Pallas kernels for 0%

profile of v1, /device:TPU:1, one launch (start us, length us, event | category | flops | bytes accessed | tf_op | source)
XLA Modules:
  0.0 576.3 jit_solution(16917837244179172518)
XLA Ops:
  7.9 3.2 copy.51
  12.6 10.8 %gather_fusion = s32[4096,2]{1,0:T(8,128)S(1)} fusion(s32[16,2]{1,0:T(8,128)S(1)} %copy.21, s32[4096]{0:T(1024)S(1)} %broadcast_clamp_fusion.1), kind=kCustom, calls=%fused_computation | custom fusion | bytes 81920 | tf_op jit(solution)/shard_map/gather | solution.py:29
  23.4 14.1 %gather_fusion.1 = s32[4096,2]{1,0:T(8,128)} fusion(s32[16,2]{1,0:T(8,128)S(1)} %copy.21, s32[4096]{0:T(1024)S(1)} %broadcast_clamp_fusion), kind=kCustom, calls=%fused_computation.1 | custom fusion | bytes 81920 | tf_op jit(solution)/shard_map/gather | solution.py:31
  40.5 7.6 %all-to-all-start = ((s32[16,1,256]{2,1,0:T(1,128)}), s32[16,1,256]{2,1,0:T(1,128)S(1)}, u32[]{:S(2)}, u32[]{:S(2)}) async-start(s32[16,1,256]{2,1,0:T(1,128)} %copy.23), calls=%async_computation | async-start | bytes 32768 | tf_op jit(solution)/shard_map/all_to_all | solution.py:97
  48.1 217.9 %while.22 = (s32[]{:T(128)}, f32[16,256,256]{2,1,0:T(8,128)}, s32[1024,32]{0,1:T(8,128)S(1)}, s32[16]{0:T(128)S(1)}, bf16[1024,256]{1,0:T(8,128)(2,1)S(1)}, /*index=5*/s32[]{:T(128)}, s32[1]{0:T(128)}) while((s32[]{:T(128)}, f32[16,256,256]{2,1,0:T(8,128)}, s32[1024,32]{0,1:T(8,128)S(1)}, s32[16]{0:T(128)S(1)}, ...), condition=%wide.region_2.3_spmd.clone, body=%wide.region_0.2_spmd.clone.sunk | while | flops 159121664 | bytes 1968245 | solution.py:94
  49.6 11.3 %convert_reduce_fusion.2 = bf16[256,1024]{1,0:T(8,128)(2,1)S(1)} fusion(s32[1024,32]{0,1:T(8,128)S(1)} %get-tuple-element.201, s32[256]{0:T(256)S(1)} %iota_add_fusion.2), kind=kLoop, calls=%fused_computation.4.clone.1 | loop fusion | flops 24903680 | bytes 656384 | tf_op jit(solution)/shard_map/while/body/eval_jaxpr/reduce_sum | solution.py:86
  63.2 11.3 %convert_reduce_fusion.2 = bf16[256,1024]{1,0:T(8,128)(2,1)S(1)} fusion(s32[1024,32]{0,1:T(8,128)S(1)} %get-tuple-element.201, s32[256]{0:T(256)S(1)} %iota_add_fusion.2), kind=kLoop, calls=%fused_computation.4.clone.1 | loop fusion | flops 24903680 | bytes 656384 | tf_op jit(solution)/shard_map/while/body/eval_jaxpr/reduce_sum | solution.py:86
  76.8 11.3 %convert_reduce_fusion.2 = bf16[256,1024]{1,0:T(8,128)(2,1)S(1)} fusion(s32[1024,32]{0,1:T(8,128)S(1)} %get-tuple-element.201, s32[256]{0:T(256)S(1)} %iota_add_fusion.2), kind=kLoop, calls=%fused_computation.4.clone.1 | loop fusion | flops 24903680 | bytes 656384 | tf_op jit(solution)/shard_map/while/body/eval_jaxpr/reduce_sum | solution.py:86
  90.4 11.3 %convert_reduce_fusion.2 = bf16[256,1024]{1,0:T(8,128)(2,1)S(1)} fusion(s32[1024,32]{0,1:T(8,128)S(1)} %get-tuple-element.201, s32[256]{0:T(256)S(1)} %iota_add_fusion.2), kind=kLoop, calls=%fused_computation.4.clone.1 | loop fusion | flops 24903680 | bytes 656384 | tf_op jit(solution)/shard_map/while/body/eval_jaxpr/reduce_sum | solution.py:86
  104.0 11.3 %convert_reduce_fusion.2 = bf16[256,1024]{1,0:T(8,128)(2,1)S(1)} fusion(s32[1024,32]{0,1:T(8,128)S(1)} %get-tuple-element.201, s32[256]{0:T(256)S(1)} %iota_add_fusion.2), kind=kLoop, calls=%fused_computation.4.clone.1 | loop fusion | flops 24903680 | bytes 656384 | tf_op jit(solution)/shard_map/while/body/eval_jaxpr/reduce_sum | solution.py:86
  117.6 11.3 %convert_reduce_fusion.2 = bf16[256,1024]{1,0:T(8,128)(2,1)S(1)} fusion(s32[1024,32]{0,1:T(8,128)S(1)} %get-tuple-element.201, s32[256]{0:T(256)S(1)} %iota_add_fusion.2), kind=kLoop, calls=%fused_computation.4.clone.1 | loop fusion | flops 24903680 | bytes 656384 | tf_op jit(solution)/shard_map/while/body/eval_jaxpr/reduce_sum | solution.py:86
  131.2 11.3 %convert_reduce_fusion.2 = bf16[256,1024]{1,0:T(8,128)(2,1)S(1)} fusion(s32[1024,32]{0,1:T(8,128)S(1)} %get-tuple-element.201, s32[256]{0:T(256)S(1)} %iota_add_fusion.2), kind=kLoop, calls=%fused_computation.4.clone.1 | loop fusion | flops 24903680 | bytes 656384 | tf_op jit(solution)/shard_map/while/body/eval_jaxpr/reduce_sum | solution.py:86
  144.8 11.3 %convert_reduce_fusion.2 = bf16[256,1024]{1,0:T(8,128)(2,1)S(1)} fusion(s32[1024,32]{0,1:T(8,128)S(1)} %get-tuple-element.201, s32[256]{0:T(256)S(1)} %iota_add_fusion.2), kind=kLoop, calls=%fused_computation.4.clone.1 | loop fusion | flops 24903680 | bytes 656384 | tf_op jit(solution)/shard_map/while/body/eval_jaxpr/reduce_sum | solution.py:86
  158.4 11.3 %convert_reduce_fusion.2 = bf16[256,1024]{1,0:T(8,128)(2,1)S(1)} fusion(s32[1024,32]{0,1:T(8,128)S(1)} %get-tuple-element.201, s32[256]{0:T(256)S(1)} %iota_add_fusion.2), kind=kLoop, calls=%fused_computation.4.clone.1 | loop fusion | flops 24903680 | bytes 656384 | tf_op jit(solution)/shard_map/while/body/eval_jaxpr/reduce_sum | solution.py:86
  172.0 11.3 %convert_reduce_fusion.2 = bf16[256,1024]{1,0:T(8,128)(2,1)S(1)} fusion(s32[1024,32]{0,1:T(8,128)S(1)} %get-tuple-element.201, s32[256]{0:T(256)S(1)} %iota_add_fusion.2), kind=kLoop, calls=%fused_computation.4.clone.1 | loop fusion | flops 24903680 | bytes 656384 | tf_op jit(solution)/shard_map/while/body/eval_jaxpr/reduce_sum | solution.py:86
  185.6 11.3 %convert_reduce_fusion.2 = bf16[256,1024]{1,0:T(8,128)(2,1)S(1)} fusion(s32[1024,32]{0,1:T(8,128)S(1)} %get-tuple-element.201, s32[256]{0:T(256)S(1)} %iota_add_fusion.2), kind=kLoop, calls=%fused_computation.4.clone.1 | loop fusion | flops 24903680 | bytes 656384 | tf_op jit(solution)/shard_map/while/body/eval_jaxpr/reduce_sum | solution.py:86
  199.2 11.3 %convert_reduce_fusion.2 = bf16[256,1024]{1,0:T(8,128)(2,1)S(1)} fusion(s32[1024,32]{0,1:T(8,128)S(1)} %get-tuple-element.201, s32[256]{0:T(256)S(1)} %iota_add_fusion.2), kind=kLoop, calls=%fused_computation.4.clone.1 | loop fusion | flops 24903680 | bytes 656384 | tf_op jit(solution)/shard_map/while/body/eval_jaxpr/reduce_sum | solution.py:86
  212.9 11.3 %convert_reduce_fusion.2 = bf16[256,1024]{1,0:T(8,128)(2,1)S(1)} fusion(s32[1024,32]{0,1:T(8,128)S(1)} %get-tuple-element.201, s32[256]{0:T(256)S(1)} %iota_add_fusion.2), kind=kLoop, calls=%fused_computation.4.clone.1 | loop fusion | flops 24903680 | bytes 656384 | tf_op jit(solution)/shard_map/while/body/eval_jaxpr/reduce_sum | solution.py:86
  226.5 11.3 %convert_reduce_fusion.2 = bf16[256,1024]{1,0:T(8,128)(2,1)S(1)} fusion(s32[1024,32]{0,1:T(8,128)S(1)} %get-tuple-element.201, s32[256]{0:T(256)S(1)} %iota_add_fusion.2), kind=kLoop, calls=%fused_computation.4.clone.1 | loop fusion | flops 24903680 | bytes 656384 | tf_op jit(solution)/shard_map/while/body/eval_jaxpr/reduce_sum | solution.py:86
  240.0 11.3 %convert_reduce_fusion.2 = bf16[256,1024]{1,0:T(8,128)(2,1)S(1)} fusion(s32[1024,32]{0,1:T(8,128)S(1)} %get-tuple-element.201, s32[256]{0:T(256)S(1)} %iota_add_fusion.2), kind=kLoop, calls=%fused_computation.4.clone.1 | loop fusion | flops 24903680 | bytes 656384 | tf_op jit(solution)/shard_map/while/body/eval_jaxpr/reduce_sum | solution.py:86
  253.6 11.3 %convert_reduce_fusion.2 = bf16[256,1024]{1,0:T(8,128)(2,1)S(1)} fusion(s32[1024,32]{0,1:T(8,128)S(1)} %get-tuple-element.201, s32[256]{0:T(256)S(1)} %iota_add_fusion.2), kind=kLoop, calls=%fused_computation.4.clone.1 | loop fusion | flops 24903680 | bytes 656384 | tf_op jit(solution)/shard_map/while/body/eval_jaxpr/reduce_sum | solution.py:86
  266.0 6.7 %all-to-all-start.1 = ((f32[16,256,256]{2,1,0:T(8,128)}), f32[16,256,256]{2,1,0:T(8,128)}, u32[]{:S(2)}, u32[]{:S(2)}) async-start(f32[16,256,256]{2,1,0:T(8,128)} %get-tuple-element.62), calls=%async_computation.1 | async-start | bytes 8388608 | tf_op jit(solution)/shard_map/all_to_all | solution.py:96
  272.8 51.8 %all-to-all-done.1 = f32[16,256,256]{2,1,0:T(8,128)} async-done(((f32[16,256,256]{2,1,0:T(8,128)}), f32[16,256,256]{2,1,0:T(8,128)}, u32[]{:S(2)}, u32[]{:S(2)}) %all-to-all-start.1) | async-done | bytes 4194336 | tf_op jit(solution)/shard_map/all_to_all | solution.py:96
  324.6 45.4 %while.23 = (s32[]{:T(128)}, f32[2048,256]{1,0:T(8,128)S(1)}, s32[16,256]{1,0:T(8,128)S(1)}, f32[16,256,256]{2,1,0:T(8,128)}, s32[]{:T(128)}, /*index=5*/s32[]{:T(128)}) while((s32[]{:T(128)}, f32[2048,256]{1,0:T(8,128)S(1)}, s32[16,256]{1,0:T(8,128)S(1)}, f32[16,256,256]{2,1,0:T(8,128)}, s32[]{:T(128)}, /*index=5*/s32[]{:T(128)}) %tuple.62), condition=%wide.region_6.7_spmd.clone, body=%wide.region_5.6_spmd.clone.sunk | while | flops 1612185600 | bytes 4459615 | solution.py:115
  327.4 2.8 convolution_add_fusion.2
  330.3 2.8 convolution_add_fusion.2
  373.5 4.6 collective-permute-start.2
  379.1 3.0 collective-permute-start.1
  388.1 165.6 %all-gather.3.cloned.1.call-done = f32[16384,256]{1,0:T(8,128)} async-done(((f32[2048,256]{1,0:T(8,128)}), f32[16384,256]{1,0:T(8,128)}) %all-gather.3.cloned.1.call-update) | async-done | bytes 16777232 | tf_op jit(solution)/shard_map/all_gather | solution.py:119
  553.7 7.1 %reduce_sum.37 = f32[2048,256]{1,0:T(8,128)S(1)} reduce(f32[8,2048,256]{2,1,0:T(8,128)} %bitcast.104, f32[]{:T(128)} %constant.105.clone.1), dimensions={0}, to_apply=%region_7.8 | reduce | flops 3670016 | bytes 18874372 | tf_op jit(solution)/shard_map/reduce_sum | solution.py:120
  561.2 2.8 psum.7
  564.6 4.8 divide_subtract_fusion
  (133 shorter events, 80.6 us)
Async XLA Ops:
  7.9 3.2 copy-start.4
  11.1 1.3 copy-start.5
  11.1 1.4 copy-start.6
  37.5 1.6 copy-start.2
  37.5 2.3 copy-start.7
  37.5 10.6 %copy-start.1 = (bf16[1024,256]{1,0:T(8,128)(2,1)S(1)}, bf16[1024,256]{1,0:T(8,128)(2,1)}, u32[]{:S(2)}) copy-start(bf16[1024,256]{1,0:T(8,128)(2,1)} %param.16) | copy-start | bytes 1572868
  37.5 10.6 %copy-start.3 = (s32[1024,32]{0,1:T(8,128)S(1)}, s32[1024,32]{0,1:T(8,128)}, u32[]{:S(2)}) copy-start(s32[1024,32]{0,1:T(8,128)} %param.17) | copy-start | bytes 393220
  40.5 225.5 %all-to-all-start = ((s32[16,1,256]{2,1,0:T(1,128)}), s32[16,1,256]{2,1,0:T(1,128)S(1)}, u32[]{:S(2)}, u32[]{:S(2)}) async-start(s32[16,1,256]{2,1,0:T(1,128)} %copy.23), calls=%async_computation | async-start | bytes 32768 | tf_op jit(solution)/shard_map/all_to_all | solution.py:97
  266.0 58.6 %all-to-all-start.1 = ((f32[16,256,256]{2,1,0:T(8,128)}), f32[16,256,256]{2,1,0:T(8,128)}, u32[]{:S(2)}, u32[]{:S(2)}) async-start(f32[16,256,256]{2,1,0:T(8,128)} %get-tuple-element.62), calls=%async_computation.1 | async-start | bytes 8388608 | tf_op jit(solution)/shard_map/all_to_all | solution.py:96
  272.7 281.0 %all-gather.3.cloned.1.call-start = ((), (), s32[]{:S(2)}) async-start(), calls=%async_computation.2 | async-start | bytes 18874368 | tf_op jit(solution)/shard_map/all_gather | solution.py:119
  370.0 1.3 copy-start
  373.5 8.7 %collective-permute-start.2 = (f32[2,64]{1,0:T(2,128)S(1)}, f32[2,64]{1,0:T(2,128)S(1)}, u32[]{:S(2)}, u32[]{:S(2)}) collective-permute-start(f32[2,64]{1,0:T(2,128)S(1)} %pad_maximum_fusion.2), channel_id=1, source_target_pairs={{0,128},{128,0},{16,144},{144,16},{32,160},{160,32},{48,176},{176,... | collective-permute-start | bytes 1544 | tf_op jit(solution)/shard_map/ppermute | solution.py:20
  379.0 5.4 collective-permute-start
  379.1 7.7 %collective-permute-start.1 = (f32[2,64,256]{2,1,0:T(8,128)S(1)}, f32[2,64,256]{2,1,0:T(8,128)S(1)}, u32[]{:S(2)}, u32[]{:S(2)}) collective-permute-start(f32[2,64,256]{2,1,0:T(8,128)S(1)} %pad_maximum_fusion.1), channel_id=1, source_target_pairs={{0,128},{128,0},{16,144},{144,16},{32,160},{160,32},{48,176},{176,... | collective-permute-start | bytes 393224 | tf_op jit(solution)/shard_map/ppermute | solution.py:20
Sparse Core Ops, SparseCore 0:
  371.5 182.1 all-gather.2
